TPU v7x, 128 devices: a whole 4x4x4 slice. The times are simulated.
128 devices in a mesh: band: 8 (over z, core), trial: 16 (over y, x).
Axes of the slice: x: 4, y: 4, z: 4, core: 2. Of those that a mesh axis runs over, the one named last changes fastest.
Arguments:
- intensity: bfloat16 [2, 16384, 4096], P(None, 'band', 'trial'), may hold values from -6 to 6
- fine_delay: int32 [32, 32, 512], P('band'), may hold values from 0 to 31
- span_start: int32 [16, 32], replicated, may hold values from 0 to 28
- sub_rel: int32 [1024, 32], P('trial'), may hold values from 0 to 3
- offset: int32 [1024, 32], P('trial'), may hold values from 0 to 2048
- widths: int32 [4], replicated, may hold values from 1 to 64
Outputs:
- series: bfloat16 [2, 1024, 4096], P(None, ('trial', 'band'))
- peaks: float32 [2, 1024, 4], P(None, ('trial', 'band'))
All inputs are finite; a program needn't handle non-finite values.
Results may differ from a plain program's by a relative error of at most 0.014.
Values may be sent and summed in bfloat16 or wider, within the bound.
A program may use at most 64 MiB of HBM per device.

v0:
```python
import math

import jax
import jax.numpy as jnp
from jax import lax
from jax.experimental import pallas as pl
from jax.experimental.pallas import tpu as pltpu
from jax.sharding import PartitionSpec as P

CH = 16384
QSPAN = 4
MAXD1 = 32
MAXD2 = 2048
LANES = 128
NT = 16
SUBS = 4
CSUB = 512
Q = 32
BLOCK = 256
ROWS = 32
PITCH = ROWS + MAXD2 // LANES + 1
MSG = 80
MESH = pl.DeviceIdType.MESH


def shift_add(first, second, step, lane):
    keep = lane < LANES - step
    low = pltpu.roll(second[1], LANES - step, 1)
    high = pltpu.roll(second[2], LANES - step, 1)
    if second[0] is None:
        early = jnp.where(keep, 0.0, low)
    else:
        early = jnp.where(keep, pltpu.roll(second[0], LANES - step, 1), low)
    if first[0] is not None:
        early = early + first[0]
    return (
        early,
        first[1] + jnp.where(keep, low, high),
        first[2] + jnp.where(keep, high, 0.0),
    )


def kernel(
    x_hbm, delay_hbm, span_ref, rel_ref, off_ref, width_ref,
    series_ref, peaks_ref,
    xv, dv, sel, lag, part, send, recv, rows, relay, chunk, half, near, total, flat, window,
    in_sem, send_sem, recv_sem, fsend_sem, frecv_sem, zsend_sem, zrecv_sem,
):
    band = lax.axis_index("band")
    me = lax.axis_index("trial")
    z = lax.div(band, 2)
    core = lax.rem(band, 2)
    sibling = band + 1 - 2 * core
    up = lax.rem(band + 2, 8)
    down = lax.rem(band + 6, 8)

    barrier = pltpu.get_barrier_semaphore()

    def greet(i, carry):
        pl.semaphore_signal(barrier, inc=1, device_id={"trial": lax.rem(me + i, NT)}, device_id_type=MESH)
        return carry

    lax.fori_loop(1, NT, greet, 0)
    for other in (sibling, up, down):
        pl.semaphore_signal(barrier, inc=1, device_id={"band": other}, device_id_type=MESH)

    def load(s):
        cut = pl.ds(s * CSUB, CSUB)
        return (
            pltpu.make_async_copy(x_hbm.at[:, cut, :], xv.at[:, cut, :], in_sem.at[0, s]),
            pltpu.make_async_copy(delay_hbm.at[s], dv.at[s], in_sem.at[1, s]),
        )

    for s in range(SUBS):
        for copy in load(s):
            copy.start()

    lane = lax.broadcasted_iota(jnp.int32, (8, LANES), 1)
    rows[...] = jnp.zeros_like(rows)
    recv[0, NT] = jnp.zeros_like(recv[0, NT])
    recv[1, NT] = jnp.zeros_like(recv[1, NT])
    flat[...] = jnp.zeros_like(flat)

    ahead = lax.broadcasted_iota(jnp.int32, (2 * LANES, LANES), 0) - lax.broadcasted_iota(
        jnp.int32, (2 * LANES, LANES), 1
    )
    for w in range(4):
        inside = (ahead >= 0) & (ahead < width_ref[w])
        window[:, w * LANES : (w + 1) * LANES] = jnp.where(inside, 1.0, 0.0).astype(jnp.bfloat16)

    for s in range(SUBS):
        for copy in load(s):
            copy.wait()
        delays = dv[s].astype(jnp.float32).astype(jnp.bfloat16)
        one = jnp.ones((), jnp.bfloat16)
        zero = jnp.zeros((), jnp.bfloat16)
        for k in range(MAXD1):
            sel[k * Q : (k + 1) * Q, :] = jnp.where(delays == jnp.bfloat16(k), one, zero)
        for b in range(2):
            lag[b] = jnp.dot(
                sel[...], xv[b, s * CSUB : (s + 1) * CSUB, :], preferred_element_type=jnp.float32
            )

        def tree(step, carry):
            b = lax.div(step, 4)
            group = lax.rem(step, 4)

            def node(level, k):
                if level == 0:
                    at = pl.ds(pl.multiple_of(k * Q + group * 8, 8), 8)
                    return (None, lag[b, at, 0:LANES], lag[b, at, LANES : 2 * LANES])
                stride = MAXD1 >> level
                return shift_add(node(level - 1, k), node(level - 1, k + stride), stride, lane)

            early, low, high = node(5, 0)
            at = pl.ds(s * 64 + group * 16 + b, 8, stride=2)
            part[0, at, :] = low
            part[1, at, :] = high
            part[2, at, :] = pltpu.roll(early, (32 * s + 32) % LANES, 1)
            return carry

        lax.fori_loop(0, 8, tree, 0)

    pl.semaphore_wait(barrier, NT + 2)

    def gather(j, put):
        for pair in range(2):
            starts = [2 * span_ref[j, band * SUBS + 2 * pair + i] + (2 * pair + i) * 64 for i in range(2)]
            for h in range(2):
                both = jnp.concatenate([part[h, pl.ds(starts[i], 8), :] for i in range(2)], axis=0)
                put(h * 32 + pair * 16, both.astype(jnp.bfloat16))
        early = part[2, pl.ds(2 * span_ref[j, band * SUBS], 8), :]
        for s in range(1, SUBS):
            early = early + part[2, pl.ds(2 * span_ref[j, band * SUBS + s] + s * 64, 8), :]
        put(64, jnp.concatenate([early, jnp.zeros_like(early)], axis=0).astype(jnp.bfloat16))

    def outgoing(i):
        return pltpu.make_async_remote_copy(
            src_ref=send.at[i], dst_ref=recv.at[core, me],
            send_sem=send_sem.at[i], recv_sem=recv_sem.at[i],
            device_id={"trial": lax.rem(me + i, NT)}, device_id_type=MESH,
        )

    def forward(i):
        source = lax.rem(me + NT - i, NT)
        return pltpu.make_async_remote_copy(
            src_ref=recv.at[core, source], dst_ref=recv.at[core, source],
            send_sem=fsend_sem.at[i], recv_sem=frecv_sem.at[i],
            device_id={"band": sibling}, device_id_type=MESH,
        )

    def send_out(i, carry):
        def put(row, value):
            send[i, row : row + 16, :] = value

        gather(lax.rem(me + i, NT), put)
        outgoing(i).start()
        return carry

    lax.fori_loop(1, NT, send_out, 0)

    def put_own(row, value):
        recv[core, me, row : row + 16, :] = value

    gather(me, put_own)
    forward(0).start()

    def pass_on(i, carry):
        outgoing(i).wait_recv()
        forward(i).start()
        return carry

    lax.fori_loop(1, NT, pass_on, 0)

    def take(i, carry):
        outgoing(i).wait_send()
        return carry

    lax.fori_loop(1, NT, take, 0)

    def arrived(i, carry):
        forward(i).wait()
        return carry

    lax.fori_loop(0, NT, arrived, 0)

    def spread(block, carry):
        for c in range(2):
            early = recv[c, block + 1, 64:80, :].astype(jnp.float32)[0:8]
            for h in range(2):
                for pair in range(2):
                    both = recv[c, block, h * 32 + pair * 16 : h * 32 + pair * 16 + 16, :].astype(jnp.float32)
                    for i in range(2):
                        s = 2 * pair + i
                        value = both[i * 8 : (i + 1) * 8]
                        if h == 1:
                            moved = pltpu.roll(early, (96 - 32 * s) % LANES, 1) if s != 3 else early
                            value = value + jnp.where(lane >= 96, moved, 0.0)
                        rows[pl.ds((c * SUBS + s) * 8 * PITCH + 2 * block + h, 8, stride=PITCH), :] = value
        return carry

    lax.fori_loop(0, NT, spread, 0)

    lane4 = lax.broadcasted_iota(jnp.int32, (ROWS, LANES), 1)

    def trial_sums(owner, g):
        at = owner * 16 + core * 8 + g
        sums = [jnp.zeros((ROWS, LANES), jnp.float32) for b in range(2)]
        for e in range(8):
            shift = off_ref[at, z * 8 + e]
            fine = jnp.bitwise_and(shift, LANES - 1)
            base = (e * 8 + 2 * rel_ref[at, z * 8 + e]) * PITCH + lax.shift_right_logical(shift, 7)
            turn = jnp.bitwise_and(LANES - fine, LANES - 1)
            for b in range(2):
                here = rows[pl.ds(base + b * PITCH, ROWS), :]
                after = rows[pl.ds(base + b * PITCH + 1, ROWS), :]
                sums[b] = sums[b] + pltpu.roll(jnp.where(lane4 >= fine, here, after), turn, 1)
        return sums

    def far(b):
        return pltpu.make_async_remote_copy(
            src_ref=chunk.at[0, b], dst_ref=relay.at[b],
            send_sem=zsend_sem.at[b], recv_sem=zrecv_sem.at[b],
            device_id={"band": up if b == 0 else down}, device_id_type=MESH,
        )

    def close(side, b):
        return pltpu.make_async_remote_copy(
            src_ref=chunk.at[1 + side, b], dst_ref=near.at[side, b],
            send_sem=zsend_sem.at[2 + 2 * side + b], recv_sem=zrecv_sem.at[2 + 2 * side + b],
            device_id={"band": up if side == 0 else down}, device_id_type=MESH,
        )

    def far_trial(g, carry):
        sums = trial_sums(lax.rem(z + 2, 4), g)
        for b in range(2):
            chunk[0, b, pl.ds(pl.multiple_of(g * ROWS, ROWS), ROWS), :] = sums[b].astype(jnp.bfloat16)
        return carry

    lax.fori_loop(0, 8, far_trial, 0)
    for b in range(2):
        far(b).start()

    for side in range(2):
        def near_trial(g, carry):
            sums = trial_sums(lax.rem(z + 1 + 2 * side, 4), g)
            at = pl.ds(pl.multiple_of(g * ROWS, ROWS), ROWS)
            half[side, at, :] = sums[side]
            chunk[1 + side, 1 - side, at, :] = sums[1 - side].astype(jnp.bfloat16)
            return carry

        lax.fori_loop(0, 8, near_trial, 0)
        close(side, 1 - side).start()

    for side in range(2):
        far(side).wait_recv()
        chunk[1 + side, side] = (half[side] + relay[side].astype(jnp.float32)).astype(jnp.bfloat16)
        close(side, side).start()

    def own_trial(g, carry):
        sums = trial_sums(z, g)
        at = pl.ds(pl.multiple_of(g * ROWS, ROWS), ROWS)
        for b in range(2):
            total[b, at, :] = sums[b]
        return carry

    lax.fori_loop(0, 8, own_trial, 0)

    for b in range(2):
        for side in (b, 1 - b)[::-1]:
            close(side, b).wait_recv()
        total[b] = (
            total[b] + (near[0, b].astype(jnp.float32) + near[1, b].astype(jnp.float32))
        ) * (1.0 / math.sqrt(CH))

    for row in range(ROWS):
        pieces = [total[b, pl.ds(row, 8, stride=ROWS), :] for b in range(2)]
        flat[row * 16 : (row + 1) * 16, :] = jnp.concatenate(pieces, axis=0).astype(jnp.bfloat16)
        for b in range(2):
            series_ref[b, :, row * LANES : (row + 1) * LANES] = pieces[b].astype(jnp.bfloat16)

    best = None
    for part_of in range(4):
        low = part_of * 128
        pair = jnp.concatenate([flat[low : low + 128, :], flat[low + 16 : low + 144, :]], axis=1)
        sums = jnp.dot(pair, window[...], preferred_element_type=jnp.float32)
        for row in range(8):
            piece = sums[row * 16 : (row + 1) * 16]
            best = piece if best is None else jnp.maximum(best, piece)
    for w in range(4):
        top = jnp.max(best[:, w * LANES : (w + 1) * LANES], axis=1, keepdims=True)
        root = jnp.sqrt(jnp.full((16, 1), width_ref[w], jnp.int32).astype(jnp.float32))
        top = top / root
        for b in range(2):
            peaks_ref[b, :, w : w + 1] = top[b * 8 : (b + 1) * 8]

    for b in range(2):
        far(b).wait_send()
        for side in range(2):
            close(side, b).wait_send()


def local(intensity, fine_delay, span_start, sub_rel, offset, widths):
    smem = pl.BlockSpec(memory_space=pltpu.SMEM)
    vmem = pl.BlockSpec(memory_space=pltpu.VMEM)
    hbm = pl.BlockSpec(memory_space=pl.ANY)
    return pl.pallas_call(
        kernel,
        out_shape=(
            jax.ShapeDtypeStruct((2, 8, ROWS * LANES), jnp.bfloat16),
            jax.ShapeDtypeStruct((2, 8, 4), jnp.float32),
        ),
        in_specs=[hbm, hbm, smem, smem, smem, smem],
        out_specs=(vmem, vmem),
        scratch_shapes=[
            pltpu.VMEM((2, SUBS * CSUB, BLOCK), jnp.bfloat16),
            pltpu.VMEM((SUBS, Q, CSUB), jnp.int32),
            pltpu.VMEM((MAXD1 * Q, CSUB), jnp.bfloat16),
            pltpu.VMEM((2, MAXD1 * Q, BLOCK), jnp.float32),
            pltpu.VMEM((3, SUBS * Q * 2, LANES), jnp.float32),
            pltpu.VMEM((NT, MSG, LANES), jnp.bfloat16),
            pltpu.VMEM((2, NT + 1, MSG, LANES), jnp.bfloat16),
            pltpu.VMEM((64 * PITCH, LANES), jnp.float32),
            pltpu.VMEM((2, 8 * ROWS, LANES), jnp.bfloat16),
            pltpu.VMEM((3, 2, 8 * ROWS, LANES), jnp.bfloat16),
            pltpu.VMEM((2, 8 * ROWS, LANES), jnp.float32),
            pltpu.VMEM((2, 2, 8 * ROWS, LANES), jnp.bfloat16),
            pltpu.VMEM((2, 8 * ROWS, LANES), jnp.float32),
            pltpu.VMEM((16 * ROWS + 16, LANES), jnp.bfloat16),
            pltpu.VMEM((2 * LANES, 4 * LANES), jnp.bfloat16),
            pltpu.SemaphoreType.DMA((2, SUBS)),
            pltpu.SemaphoreType.DMA((NT,)),
            pltpu.SemaphoreType.DMA((NT,)),
            pltpu.SemaphoreType.DMA((NT,)),
            pltpu.SemaphoreType.DMA((NT,)),
            pltpu.SemaphoreType.DMA((6,)),
            pltpu.SemaphoreType.DMA((6,)),
        ],
        compiler_params=pltpu.CompilerParams(
            collective_id=0, has_side_effects=True, vmem_limit_bytes=40 * 1024 * 1024
        ),
        name="dedisperse",
    )(intensity, fine_delay, span_start, sub_rel, offset, widths)


def solution(mesh):
    return jax.shard_map(
        local,
        mesh=mesh,
        in_specs=(
            P(None, "band", "trial"),
            P("band", None, None),
            P(),
            P("trial", None),
            P("trial", None),
            P(),
        ),
        out_specs=(P(None, ("trial", "band"), None), P(None, ("trial", "band"), None)),
        check_vma=False,
    )
```

profile of v0, /device:TPU:1, one launch (start us, length us, event | category | flops | bytes accessed | tf_op | source)
XLA Modules:
  0.0 49.0 jit_solution(8716099453289115094)
XLA Ops:
  0.6 0.8 %copy.8.rel_ref = s32[64,32]{1,0:T(8,128)S(1)} copy(s32[64,32]{0,1:T(8,128)} %param.9) | data formatting | bytes 16384 | tf_op args[3]
  1.4 0.8 %copy.9.off_ref = s32[64,32]{1,0:T(8,128)S(1)} copy(s32[64,32]{0,1:T(8,128)} %param.10) | data formatting | bytes 16384 | tf_op args[4]
  2.2 0.0 copy-start
  2.2 1.6 %copy-done = bf16[2,2048,256]{2,1,0:T(8,128)(2,1)S(1)} copy-done((bf16[2,2048,256]{2,1,0:T(8,128)(2,1)S(1)}, bf16[2,2048,256]{2,1,0:T(8,128)(2,1)}, u32[]{:S(2)}) %copy-start) | copy-done | bytes 2097176
  3.8 0.0 copy-start.1
  3.8 0.9 %copy-done.1 = s32[4,32,512]{2,1,0:T(8,128)S(1)} copy-done((s32[4,32,512]{2,1,0:T(8,128)S(1)}, s32[4,32,512]{2,1,0:T(8,128)}, u32[]{:S(2)}) %copy-start.1) | copy-done | bytes 262168
  4.8 0.0 copy-start.2
  4.8 0.7 %copy-done.2 = s32[16,32]{1,0:T(8,128)S(1)} copy-done((s32[16,32]{1,0:T(8,128)S(1)}, s32[16,32]{1,0:T(8,128)}, u32[]{:S(2)}) %copy-start.2) | copy-done | bytes 2072
  5.5 0.0 copy-start.3
  5.5 0.7 %copy-done.3 = s32[4]{0:T(128)S(1)} copy-done((s32[4]{0:T(128)S(1)}, s32[4]{0:T(128)}, u32[]{:S(2)}) %copy-start.3) | copy-done | bytes 40
  6.1 41.6 %dedisperse.1 = (bf16[2,8,4096]{2,1,0:T(8,128)(2,1)S(1)}, f32[2,8,4]{2,1,0:T(8,128)S(1)}) custom-call(bf16[2,2048,256]{2,1,0:T(8,128)(2,1)S(1)} %copy-done, s32[4,32,512]{2,1,0:T(8,128)S(1)} %copy-done.1, s32[16,32]{1,0:T(8,128)S(1)} %copy-done.2, s32[64,32]{1,0:T(8,128)S(1)} %copy.8.rel_ref, s32[64,32]{1,0:T(8,128)S(1)} %copy.9.off_ref, s32[4]{0:T(128)S(1)} %copy-done.3), custom_call_target="tpu_custom_call" | custom-call | tf_op jit(solution)/shard_map/dedisperse/pallas_call | solution.py:307
  47.7 0.7 %copy.10 = f32[2,8,4]{1,2,0:T(4,128)} copy(f32[2,8,4]{2,1,0:T(8,128)S(1)} %get-tuple-element.3) | data formatting | bytes 512 | tf_op jit(solution)/shard_map/dedisperse/pallas_call | solution.py:307
  48.4 0.7 %copy.12 = bf16[2,8,4096]{2,1,0:T(8,128)(2,1)} copy(bf16[2,8,4096]{2,1,0:T(8,128)(2,1)S(1)} %get-tuple-element.6) | data formatting | bytes 262144
Async XLA Ops:
  2.2 1.6 %copy-start = (bf16[2,2048,256]{2,1,0:T(8,128)(2,1)S(1)}, bf16[2,2048,256]{2,1,0:T(8,128)(2,1)}, u32[]{:S(2)}) copy-start(bf16[2,2048,256]{2,1,0:T(8,128)(2,1)} %x_hbm.1) | copy-start | bytes 6291460
  3.8 0.9 %copy-start.1 = (s32[4,32,512]{2,1,0:T(8,128)S(1)}, s32[4,32,512]{2,1,0:T(8,128)}, u32[]{:S(2)}) copy-start(s32[4,32,512]{2,1,0:T(8,128)} %delay_hbm.1) | copy-start | bytes 786436
  4.8 0.7 %copy-start.2 = (s32[16,32]{1,0:T(8,128)S(1)}, s32[16,32]{1,0:T(8,128)}, u32[]{:S(2)}) copy-start(s32[16,32]{1,0:T(8,128)} %span_ref.1) | copy-start | bytes 6148
  5.5 0.7 %copy-start.3 = (s32[4]{0:T(128)S(1)}, s32[4]{0:T(128)}, u32[]{:S(2)}) copy-start(s32[4]{0:T(128)} %width_ref.1) | copy-start | bytes 52
where the time goes:
time: 49.5 us; the launch traced here: 49 us
  Pallas kernels  41.6 us (84%)
  local copies, waits for them, and re-layouts  6.82 us (14%)
  between operations  0.65 us (1%)
    pallas_call x1, Pallas kernels, local(): pl.pallas_call(kernel, out_shape=(jax.ShapeDtypeStruct((2, 8, ROWS * LANE...  41.6 us
    unnamed x11, local copies, waits for them, and re-layouts  6.14 us

commit v1 on v0

--- a/solution.py
+++ b/solution.py
@@ -21,6 +21,15 @@
 PITCH = ROWS + MAXD2 // LANES + 1
 MSG = 80
 MESH = pl.DeviceIdType.MESH
+
+
+def leaves(level, k):
+    if level == 0:
+        return [k]
+    return leaves(level - 1, k) + leaves(level - 1, k + (MAXD1 >> level))
+
+
+LEAVES = leaves(5, 0)
 
 
 def shift_add(first, second, step, lane):
@@ -41,10 +50,10 @@
 
 
 def kernel(
-    x_hbm, delay_hbm, span_ref, rel_ref, off_ref, width_ref,
+    x_hbm, delay_hbm, span_hbm, rel_hbm, off_hbm, width_hbm,
     series_ref, peaks_ref,
-    xv, dv, sel, lag, part, send, recv, rows, relay, chunk, half, near, total, flat, window,
-    in_sem, send_sem, recv_sem, fsend_sem, frecv_sem, zsend_sem, zrecv_sem,
+    xv, dv, span_ref, rel_ref, off_ref, width_ref, lag, part, send, recv, rows, relay, chunk, half, near, total, flat, window,
+    in_sem, small_sem, send_sem, recv_sem, fsend_sem, frecv_sem, zsend_sem, zrecv_sem,
 ):
     band = lax.axis_index("band")
     me = lax.axis_index("trial")
@@ -75,11 +84,114 @@
         for copy in load(s):
             copy.start()
 
+    own_bands = pl.ds(pl.multiple_of(z * 8, 8), 8)
+    small = [
+        pltpu.make_async_copy(span_hbm, span_ref, small_sem.at[0]),
+        pltpu.make_async_copy(rel_hbm.at[own_bands, :], rel_ref, small_sem.at[1]),
+        pltpu.make_async_copy(off_hbm.at[own_bands, :], off_ref, small_sem.at[2]),
+        pltpu.make_async_copy(width_hbm, width_ref, small_sem.at[3]),
+    ]
+    for copy in small:
+        copy.start()
+
     lane = lax.broadcasted_iota(jnp.int32, (8, LANES), 1)
     rows[...] = jnp.zeros_like(rows)
     recv[0, NT] = jnp.zeros_like(recv[0, NT])
     recv[1, NT] = jnp.zeros_like(recv[1, NT])
     flat[...] = jnp.zeros_like(flat)
+
+    group = lax.broadcasted_iota(jnp.int32, (8, LANES), 1) // Q
+    lag[:, :, 0:8, :] = jnp.zeros((8, 2, 8, LANES), jnp.float32)
+    lag[:, :, 8 + BLOCK :, :] = jnp.zeros((8, 2, 8, LANES), jnp.float32)
+    one = jnp.ones((), jnp.bfloat16)
+    zero = jnp.zeros((), jnp.bfloat16)
+    for s in range(SUBS):
+        for copy in load(s):
+            copy.wait()
+        times = jnp.concatenate(
+            [xv[b, s * CSUB : (s + 1) * CSUB, :].T for b in range(2)], axis=0
+        )
+        delays = dv[s].astype(jnp.float32)
+        delays = jnp.concatenate([delays - 8.0 * j for j in range(4)], axis=0).T.astype(jnp.bfloat16)
+        for m in range(0, 8, 2):
+            sel = jnp.concatenate(
+                [jnp.where(delays == jnp.bfloat16(m + i), one, zero) for i in range(2)], axis=1
+            )
+            product = jnp.dot(times, sel, preferred_element_type=jnp.float32)
+            for i in range(2):
+                for b in range(2):
+                    lag[m + i, b, 8 : 8 + BLOCK, :] = product[
+                        b * BLOCK : (b + 1) * BLOCK, i * LANES : (i + 1) * LANES
+                    ]
+        for b in range(2):
+            sums = []
+            for v in range(BLOCK // 8 + 1):
+                add = lag[0, b, 8 * v : 8 * v + 8, :]
+                for m in range(1, 8):
+                    add = add + lag[m, b, 8 * v + m : 8 * v + m + 8, :]
+                sums.append(add)
+
+            def at(v):
+                return sums[v] if 0 <= v < len(sums) else jnp.zeros((8, LANES), jnp.float32)
+
+            lined = []
+            for v in range(-3, BLOCK // 8 + 1):
+                line = at(v)
+                for j in range(1, 4):
+                    line = jnp.where(group == j, at(v + j), line)
+                lined.append(line)
+            lined = [jnp.zeros((8, LANES), jnp.float32)] * 12 + lined
+            for tile in range(3):
+                turned = jnp.concatenate(lined[16 * tile : 16 * tile + 16], axis=0).T
+                folded = (turned[0:32] + turned[32:64]) + (turned[64:96] + turned[96:128])
+                part[(tile + 2) % 3, pl.ds(s * 64 + b, 32, stride=2), :] = folded
+
+    for copy in small:
+        copy.wait()
+    pl.semaphore_wait(barrier, NT + 2)
+
+    def gather(j, put):
+        for pair in range(2):
+            starts = [2 * span_ref[j, band * SUBS + 2 * pair + i] + (2 * pair + i) * 64 for i in range(2)]
+            for h in range(2):
+                both = jnp.concatenate([part[h, pl.ds(starts[i], 8), :] for i in range(2)], axis=0)
+                put(h * 32 + pair * 16, both.astype(jnp.bfloat16))
+        early = part[2, pl.ds(2 * span_ref[j, band * SUBS + 3] + 192, 8), :]
+        for s in range(3):
+            more = part[2, pl.ds(2 * span_ref[j, band * SUBS + s] + s * 64, 8), :]
+            early = early + pltpu.roll(more, 32 * s + 32, 1)
+        put(64, jnp.concatenate([early, jnp.zeros_like(early)], axis=0).astype(jnp.bfloat16))
+
+    def outgoing(i):
+        return pltpu.make_async_remote_copy(
+            src_ref=send.at[i], dst_ref=recv.at[core, me],
+            send_sem=send_sem.at[i], recv_sem=recv_sem.at[i],
+            device_id={"trial": lax.rem(me + i, NT)}, device_id_type=MESH,
+        )
+
+    def forward(i):
+        source = lax.rem(me + NT - i, NT)
+        return pltpu.make_async_remote_copy(
+            src_ref=recv.at[core, source], dst_ref=recv.at[core, source],
+            send_sem=fsend_sem.at[i], recv_sem=frecv_sem.at[i],
+            device_id={"band": sibling}, device_id_type=MESH,
+        )
+
+    def send_out(i, carry):
+        def put(row, value):
+            send[i, row : row + 16, :] = value
+
+        gather(lax.rem(me + i, NT), put)
+        outgoing(i).start()
+        return carry
+
+    lax.fori_loop(1, NT, send_out, 0)
+
+    def put_own(row, value):
+        recv[core, me, row : row + 16, :] = value
+
+    gather(me, put_own)
+    forward(0).start()
 
     ahead = lax.broadcasted_iota(jnp.int32, (2 * LANES, LANES), 0) - lax.broadcasted_iota(
         jnp.int32, (2 * LANES, LANES), 1
@@ -87,83 +199,6 @@
     for w in range(4):
         inside = (ahead >= 0) & (ahead < width_ref[w])
         window[:, w * LANES : (w + 1) * LANES] = jnp.where(inside, 1.0, 0.0).astype(jnp.bfloat16)
-
-    for s in range(SUBS):
-        for copy in load(s):
-            copy.wait()
-        delays = dv[s].astype(jnp.float32).astype(jnp.bfloat16)
-        one = jnp.ones((), jnp.bfloat16)
-        zero = jnp.zeros((), jnp.bfloat16)
-        for k in range(MAXD1):
-            sel[k * Q : (k + 1) * Q, :] = jnp.where(delays == jnp.bfloat16(k), one, zero)
-        for b in range(2):
-            lag[b] = jnp.dot(
-                sel[...], xv[b, s * CSUB : (s + 1) * CSUB, :], preferred_element_type=jnp.float32
-            )
-
-        def tree(step, carry):
-            b = lax.div(step, 4)
-            group = lax.rem(step, 4)
-
-            def node(level, k):
-                if level == 0:
-                    at = pl.ds(pl.multiple_of(k * Q + group * 8, 8), 8)
-                    return (None, lag[b, at, 0:LANES], lag[b, at, LANES : 2 * LANES])
-                stride = MAXD1 >> level
-                return shift_add(node(level - 1, k), node(level - 1, k + stride), stride, lane)
-
-            early, low, high = node(5, 0)
-            at = pl.ds(s * 64 + group * 16 + b, 8, stride=2)
-            part[0, at, :] = low
-            part[1, at, :] = high
-            part[2, at, :] = pltpu.roll(early, (32 * s + 32) % LANES, 1)
-            return carry
-
-        lax.fori_loop(0, 8, tree, 0)
-
-    pl.semaphore_wait(barrier, NT + 2)
-
-    def gather(j, put):
-        for pair in range(2):
-            starts = [2 * span_ref[j, band * SUBS + 2 * pair + i] + (2 * pair + i) * 64 for i in range(2)]
-            for h in range(2):
-                both = jnp.concatenate([part[h, pl.ds(starts[i], 8), :] for i in range(2)], axis=0)
-                put(h * 32 + pair * 16, both.astype(jnp.bfloat16))
-        early = part[2, pl.ds(2 * span_ref[j, band * SUBS], 8), :]
-        for s in range(1, SUBS):
-            early = early + part[2, pl.ds(2 * span_ref[j, band * SUBS + s] + s * 64, 8), :]
-        put(64, jnp.concatenate([early, jnp.zeros_like(early)], axis=0).astype(jnp.bfloat16))
-
-    def outgoing(i):
-        return pltpu.make_async_remote_copy(
-            src_ref=send.at[i], dst_ref=recv.at[core, me],
-            send_sem=send_sem.at[i], recv_sem=recv_sem.at[i],
-            device_id={"trial": lax.rem(me + i, NT)}, device_id_type=MESH,
-        )
-
-    def forward(i):
-        source = lax.rem(me + NT - i, NT)
-        return pltpu.make_async_remote_copy(
-            src_ref=recv.at[core, source], dst_ref=recv.at[core, source],
-            send_sem=fsend_sem.at[i], recv_sem=frecv_sem.at[i],
-            device_id={"band": sibling}, device_id_type=MESH,
-        )
-
-    def send_out(i, carry):
-        def put(row, value):
-            send[i, row : row + 16, :] = value
-
-        gather(lax.rem(me + i, NT), put)
-        outgoing(i).start()
-        return carry
-
-    lax.fori_loop(1, NT, send_out, 0)
-
-    def put_own(row, value):
-        recv[core, me, row : row + 16, :] = value
-
-    gather(me, put_own)
-    forward(0).start()
 
     def pass_on(i, carry):
         outgoing(i).wait_recv()
@@ -207,9 +242,9 @@
         at = owner * 16 + core * 8 + g
         sums = [jnp.zeros((ROWS, LANES), jnp.float32) for b in range(2)]
         for e in range(8):
-            shift = off_ref[at, z * 8 + e]
+            shift = off_ref[e, at]
             fine = jnp.bitwise_and(shift, LANES - 1)
-            base = (e * 8 + 2 * rel_ref[at, z * 8 + e]) * PITCH + lax.shift_right_logical(shift, 7)
+            base = (e * 8 + 2 * rel_ref[e, at]) * PITCH + lax.shift_right_logical(shift, 7)
             turn = jnp.bitwise_and(LANES - fine, LANES - 1)
             for b in range(2):
                 here = rows[pl.ds(base + b * PITCH, ROWS), :]
@@ -301,22 +336,24 @@
 
 
 def local(intensity, fine_delay, span_start, sub_rel, offset, widths):
-    smem = pl.BlockSpec(memory_space=pltpu.SMEM)
     vmem = pl.BlockSpec(memory_space=pltpu.VMEM)
-    hbm = pl.BlockSpec(memory_space=pl.ANY)
+    hbm = pl.BlockSpec(memory_space=pltpu.HBM)
     return pl.pallas_call(
         kernel,
         out_shape=(
             jax.ShapeDtypeStruct((2, 8, ROWS * LANES), jnp.bfloat16),
             jax.ShapeDtypeStruct((2, 8, 4), jnp.float32),
         ),
-        in_specs=[hbm, hbm, smem, smem, smem, smem],
+        in_specs=[hbm] * 6,
         out_specs=(vmem, vmem),
         scratch_shapes=[
             pltpu.VMEM((2, SUBS * CSUB, BLOCK), jnp.bfloat16),
             pltpu.VMEM((SUBS, Q, CSUB), jnp.int32),
-            pltpu.VMEM((MAXD1 * Q, CSUB), jnp.bfloat16),
-            pltpu.VMEM((2, MAXD1 * Q, BLOCK), jnp.float32),
+            pltpu.SMEM((NT, 32), jnp.int32),
+            pltpu.SMEM((8, 64), jnp.int32),
+            pltpu.SMEM((8, 64), jnp.int32),
+            pltpu.SMEM((4,), jnp.int32),
+            pltpu.VMEM((8, 2, BLOCK + 16, LANES), jnp.float32),
             pltpu.VMEM((3, SUBS * Q * 2, LANES), jnp.float32),
             pltpu.VMEM((NT, MSG, LANES), jnp.bfloat16),
             pltpu.VMEM((2, NT + 1, MSG, LANES), jnp.bfloat16),
@@ -329,6 +366,7 @@
             pltpu.VMEM((16 * ROWS + 16, LANES), jnp.bfloat16),
             pltpu.VMEM((2 * LANES, 4 * LANES), jnp.bfloat16),
             pltpu.SemaphoreType.DMA((2, SUBS)),
+            pltpu.SemaphoreType.DMA((4,)),
             pltpu.SemaphoreType.DMA((NT,)),
             pltpu.SemaphoreType.DMA((NT,)),
             pltpu.SemaphoreType.DMA((NT,)),
@@ -337,10 +375,10 @@
             pltpu.SemaphoreType.DMA((6,)),
         ],
         compiler_params=pltpu.CompilerParams(
-            collective_id=0, has_side_effects=True, vmem_limit_bytes=40 * 1024 * 1024
+            collective_id=0, has_side_effects=True, vmem_limit_bytes=67043328
         ),
         name="dedisperse",
-    )(intensity, fine_delay, span_start, sub_rel, offset, widths)
+    )(intensity, fine_delay, span_start, sub_rel.T, offset.T, widths)
 
 
 def solution(mesh):

time: 49.5 us -> 33.3 us (0.67)
  Pallas kernels: 41.6 us -> 29.4 us
  local copies, waits for them, and re-layouts: 6.82 us -> 2.94 us
    pallas_call x1, Pallas kernels: 41.6 us -> 29.4 us  [local(): pl.pallas_call(kernel, out_shape=(jax.ShapeDtypeStruct((2, 8, ROWS * LANE...]
    unnamed x11 -> x1, local copies, waits for them, and re-layouts: 6.14 us -> 1.57 us
    pallas_call x1, local copies, waits for them, and re-layouts: 0.67 us -> 1.37 us  [local(): pl.pallas_call(kernel, out_shape=(jax.ShapeDtypeStruct((2, 8, ROWS * LANE...]
where the time goes in v1:
time: 33.3 us; the launch traced here: 32.9 us
  Pallas kernels  29.4 us (88%)
  local copies, waits for them, and re-layouts  2.94 us (9%)
  between operations  0.64 us (2%)
    pallas_call x1, Pallas kernels, local(): pl.pallas_call(kernel, out_shape=(jax.ShapeDtypeStruct((2, 8, ROWS * LANE...  29.4 us
    unnamed x1, local copies, waits for them, and re-layouts  1.57 us
    pallas_call x1, local copies, waits for them, and re-layouts, local(): pl.pallas_call(kernel, out_shape=(jax.ShapeDtypeStruct((2, 8, ROWS * LANE...  1.37 us

profile of v1, /device:TPU:1, one launch (start us, length us, event | category | flops | bytes accessed | tf_op | source)
XLA Modules:
  0.0 32.9 jit_solution(17274012100696769964)
XLA Ops:
  0.6 29.4 %dedisperse.1 = (bf16[2,8,4096]{2,1,0:T(8,128)(2,1)}, f32[2,8,4]{2,1,0:T(8,128)}) custom-call(bf16[2,2048,256]{2,1,0:T(8,128)(2,1)} %x_hbm.1, s32[4,32,512]{2,1,0:T(8,128)} %delay_hbm.1, s32[16,32]{1,0:T(8,128)} %span_hbm.1, s32[32,64]{1,0:T(8,128)} %bitcast.2, s32[32,64]{1,0:T(8,128)} %bitcast.3, s32[4]{0:T(128)} %width_hbm.1), custom_call_target="tpu_custom_call" | custom-call | tf_op jit(solution)/shard_map/dedisperse/pallas_call | solution.py:341
  30.0 1.4 %copy.8 = f32[2,8,4]{1,2,0:T(4,128)} copy(f32[2,8,4]{2,1,0:T(8,128)} %get-tuple-element.3) | data formatting | bytes 512 | tf_op jit(solution)/shard_map/dedisperse/pallas_call | solution.py:341
  31.4 1.6 %copy.10 = bf16[2,8,4096]{2,1,0:T(8,128)(2,1)} copy(bf16[2,8,4096]{2,1,0:T(8,128)(2,1)} %get-tuple-element.6) | data formatting | bytes 262144

commit v2 on v1

v2 whole, which is shorter than its diff:
```python
import math

import jax
import jax.numpy as jnp
from jax import lax
from jax.experimental import pallas as pl
from jax.experimental.pallas import tpu as pltpu
from jax.sharding import PartitionSpec as P

CH = 16384
QSPAN = 4
MAXD1 = 32
MAXD2 = 2048
LANES = 128
NT = 16
SUBS = 4
CSUB = 512
Q = 32
BLOCK = 256
ROWS = 32
PITCH = ROWS + MAXD2 // LANES + 1
MSG = 80
VMEM_MIB = 32
FAR_FIRST = (10, 9, 11, 6, 14, 8, 2, 5, 7, 13, 15, 12, 4, 1, 3)
MESH = pl.DeviceIdType.MESH


def leaves(level, k):
    if level == 0:
        return [k]
    return leaves(level - 1, k) + leaves(level - 1, k + (MAXD1 >> level))


LEAVES = leaves(5, 0)


def shift_add(first, second, step, lane):
    keep = lane < LANES - step
    low = pltpu.roll(second[1], LANES - step, 1)
    high = pltpu.roll(second[2], LANES - step, 1)
    if second[0] is None:
        early = jnp.where(keep, 0.0, low)
    else:
        early = jnp.where(keep, pltpu.roll(second[0], LANES - step, 1), low)
    if first[0] is not None:
        early = early + first[0]
    return (
        early,
        first[1] + jnp.where(keep, low, high),
        first[2] + jnp.where(keep, high, 0.0),
    )


def kernel(
    x_hbm, delay_hbm, span_hbm, rel_hbm, off_hbm, width_hbm,
    total, near, window, roots,
    xv, dv, span_ref, rel_ref, off_ref, width_ref, lag, part, send, recv, rows, relay, chunk, half, acc,
    in_sem, small_sem, send_sem, recv_sem, fsend_sem, frecv_sem, zsend_sem, zrecv_sem,
):
    band = lax.axis_index("band")
    me = lax.axis_index("trial")
    z = lax.div(band, 2)
    core = lax.rem(band, 2)
    sibling = band + 1 - 2 * core
    up = lax.rem(band + 2, 8)
    down = lax.rem(band + 6, 8)

    barrier = pltpu.get_barrier_semaphore()

    def load(s):
        cut = pl.ds(s * CSUB, CSUB)
        return (
            pltpu.make_async_copy(x_hbm.at[:, cut, :], xv.at[:, cut, :], in_sem.at[0, s]),
            pltpu.make_async_copy(delay_hbm.at[s], dv.at[s], in_sem.at[1, s]),
        )

    for s in range(SUBS):
        for copy in load(s):
            copy.start()

    def greet(i, carry):
        pl.semaphore_signal(barrier, inc=1, device_id={"trial": lax.rem(me + i, NT)}, device_id_type=MESH)
        return carry

    lax.fori_loop(1, NT, greet, 0)
    for other in (sibling, up, down):
        pl.semaphore_signal(barrier, inc=1, device_id={"band": other}, device_id_type=MESH)

    own_bands = pl.ds(pl.multiple_of(z * 8, 8), 8)
    small = [
        pltpu.make_async_copy(span_hbm, span_ref, small_sem.at[0]),
        pltpu.make_async_copy(rel_hbm.at[own_bands, :], rel_ref, small_sem.at[1]),
        pltpu.make_async_copy(off_hbm.at[own_bands, :], off_ref, small_sem.at[2]),
        pltpu.make_async_copy(width_hbm, width_ref, small_sem.at[3]),
    ]
    for copy in small:
        copy.start()

    lane = lax.broadcasted_iota(jnp.int32, (8, LANES), 1)
    rows[...] = jnp.zeros_like(rows)
    recv[0, NT] = jnp.zeros_like(recv[0, NT])
    recv[1, NT] = jnp.zeros_like(recv[1, NT])

    def gather(pair, j, put):
        starts = [2 * span_ref[j, band * SUBS + 2 * pair + i] + (2 * pair + i) * 64 for i in range(2)]
        for h in range(2):
            both = [part[h, pl.ds(start, 8), :] for start in starts]
            put(pair * 40 + h * 16, jnp.concatenate(both, axis=0).astype(jnp.bfloat16))
        early = [part[2, pl.ds(start, 8), :] for start in starts]
        put(pair * 40 + 32, (pltpu.roll(early[0], 96, 1) + early[1]).astype(jnp.bfloat16))

    def outgoing(pair, i):
        cut = pl.ds(pair * 40, 40)
        return pltpu.make_async_remote_copy(
            src_ref=send.at[i, cut, :], dst_ref=recv.at[core, me, cut, :],
            send_sem=send_sem.at[pair, i], recv_sem=recv_sem.at[pair, i],
            device_id={"trial": lax.rem(me + i, NT)}, device_id_type=MESH,
        )

    def send_pair(pair):
        for i in FAR_FIRST:

            def put(row, value):
                send[i, row : row + value.shape[0], :] = value

            gather(pair, lax.rem(me + i, NT), put)
            outgoing(pair, i).start()

        def put_own(row, value):
            recv[core, me, row : row + value.shape[0], :] = value

        gather(pair, me, put_own)

    group = lax.broadcasted_iota(jnp.int32, (8, LANES), 1) // Q
    blank = jnp.zeros((8, LANES), jnp.float32)
    lag[:, :, :, 0:8, :] = jnp.zeros((2, 8, 2, 8, LANES), jnp.float32)
    lag[:, :, :, 8 + BLOCK :, :] = jnp.zeros((2, 8, 2, 8, LANES), jnp.float32)
    one = jnp.ones((), jnp.bfloat16)
    zero = jnp.zeros((), jnp.bfloat16)

    times, lagged = {}, {}

    def turn_data(s, b):
        times[s, b] = xv[b, s * CSUB : (s + 1) * CSUB, :].T

    def turn_delays(s):
        delays = dv[s].astype(jnp.float32)
        delays = jnp.concatenate([delays - 8.0 * j for j in range(4)], axis=0)
        lagged[s] = delays.T.astype(jnp.bfloat16)

    def product(s, m):
        delays = lagged[s]
        sel = jnp.concatenate(
            [jnp.where(delays == jnp.bfloat16(m + i), one, zero) for i in range(2)], axis=1
        )
        result = jnp.dot(jnp.concatenate([times[s, 0], times[s, 1]], axis=0), sel, preferred_element_type=jnp.float32)
        for i in range(2):
            for b in range(2):
                lag[s % 2, m + i, b, 8 : 8 + BLOCK, :] = result[
                    b * BLOCK : (b + 1) * BLOCK, i * LANES : (i + 1) * LANES
                ]

    def fold(s, b):
        sums = {}

        def at(v):
            if not 0 <= v <= BLOCK // 8:
                return blank
            if v not in sums:
                add = lag[s % 2, 0, b, 8 * v : 8 * v + 8, :]
                for m in range(1, 8):
                    add = add + lag[s % 2, m, b, 8 * v + m : 8 * v + m + 8, :]
                sums[v] = add
            return sums[v]

        def line(v):
            if v < -3:
                return blank
            picked = at(v)
            for j in range(1, 4):
                picked = jnp.where(group == j, at(v + j), picked)
            return picked

        for tile in range(3):
            turned = jnp.concatenate([line(16 * tile - 15 + i) for i in range(16)], axis=0).T
            folded = (turned[0:32] + turned[32:64]) + (turned[64:96] + turned[96:128])
            part[(tile + 2) % 3, pl.ds(s * 64 + b, 32, stride=2), :] = folded

    def arrive(s):
        for copy in load(s):
            copy.wait()

    arrive(0)
    turn_data(0, 0)
    turn_data(0, 1)
    turn_delays(0)
    for s in range(SUBS):
        if s + 1 < SUBS:
            arrive(s + 1)
        product(s, 0)
        if s % 2 == 1:
            fold(s - 1, 0)
        product(s, 2)
        if s + 1 < SUBS:
            turn_data(s + 1, 0)
        product(s, 4)
        if s % 2 == 1:
            fold(s - 1, 1)
        product(s, 6)
        if s + 1 < SUBS:
            turn_data(s + 1, 1)
            turn_delays(s + 1)
        if s % 2 == 1:
            fold(s, 0)
            fold(s, 1)
            if s == 1:
                for copy in small:
                    copy.wait()
                pl.semaphore_wait(barrier, NT + 2)
            send_pair(s // 2)

    def forward(pair):
        cut = (core, pl.ds(0, NT), pl.ds(pair * 40, 40))
        return pltpu.make_async_remote_copy(
            src_ref=recv.at[cut], dst_ref=recv.at[cut],
            send_sem=fsend_sem.at[pair], recv_sem=frecv_sem.at[pair],
            device_id={"band": sibling}, device_id_type=MESH,
        )

    def collect(pair):
        def wait_one(i, carry):
            outgoing(pair, i).wait_recv()
            return carry

        lax.fori_loop(1, NT, wait_one, 0)
        forward(pair).start()

    def spread(c, pair):
        def one_block(block, carry):
            early = recv[c, block + 1, pair * 40 + 32 : pair * 40 + 40, :].astype(jnp.float32)
            for h in range(2):
                both = recv[c, block, pair * 40 + h * 16 : pair * 40 + h * 16 + 16, :].astype(jnp.float32)
                for i in range(2):
                    value = both[i * 8 : (i + 1) * 8]
                    if h == 1:
                        moved = pltpu.roll(early, 32, 1) if i == 0 else early
                        value = value + jnp.where(lane >= 96, moved, 0.0)
                    rows[pl.ds((c * SUBS + 2 * pair + i) * 8 * PITCH + 2 * block + h, 8, stride=PITCH), :] = value
            return carry

        lax.fori_loop(0, NT, one_block, 0, unroll=4)

    ahead = lax.broadcasted_iota(jnp.int32, (2 * LANES, LANES), 0) - lax.broadcasted_iota(
        jnp.int32, (2 * LANES, LANES), 1
    )
    for w in range(4):
        inside = (ahead >= 0) & (ahead < width_ref[w])
        window[:, w * LANES : (w + 1) * LANES] = jnp.where(inside, 1.0, 0.0).astype(jnp.bfloat16)
        root = jnp.sqrt(jnp.full((8, LANES), width_ref[w], jnp.int32).astype(jnp.float32))
        roots[:, w * LANES : (w + 1) * LANES] = root

    lane8 = lax.broadcasted_iota(jnp.int32, (2 * ROWS, LANES), 1)

    def trial_sums(owner, g, subs):
        at = owner * 16 + core * 8 + g
        sums = None
        for e in subs:
            shift = off_ref[e, at]
            fine = jnp.bitwise_and(shift, LANES - 1)
            base = (e * 8 + 2 * rel_ref[e, at]) * PITCH + lax.shift_right_logical(shift, 7)
            turn = jnp.bitwise_and(LANES - fine, LANES - 1)
            here, after = [
                jnp.concatenate([rows[pl.ds(base + b * PITCH + next_row, ROWS), :] for b in range(2)], axis=0)
                for next_row in range(2)
            ]
            joined = jnp.where(lane8 >= fine, here, after).astype(jnp.bfloat16)
            moved = pltpu.roll(joined, turn, 1).astype(jnp.float32)
            sums = moved if sums is None else sums + moved
        return sums

    def piece(b, p):
        return {"band": up if b == 0 else down}, pl.ds(p * 4 * ROWS, 4 * ROWS)

    def far(b, p):
        where, cut = piece(b, p)
        return pltpu.make_async_remote_copy(
            src_ref=chunk.at[0, b, cut, :], dst_ref=relay.at[b, cut, :],
            send_sem=zsend_sem.at[2 * b + p], recv_sem=zrecv_sem.at[2 * b + p],
            device_id=where, device_id_type=MESH,
        )

    def close(side, p):
        where, cut = piece(side, p)
        return pltpu.make_async_remote_copy(
            src_ref=chunk.at[1 + side, side, cut, :], dst_ref=near.at[side, side, cut, :],
            send_sem=zsend_sem.at[4 + 2 * side + p], recv_sem=zrecv_sem.at[4 + 2 * side + p],
            device_id=where, device_id_type=MESH,
        )

    def direct(side):
        return pltpu.make_async_remote_copy(
            src_ref=chunk.at[1 + side, 1 - side], dst_ref=near.at[side, 1 - side],
            send_sem=zsend_sem.at[8 + side], recv_sem=zrecv_sem.at[8 + side],
            device_id={"band": up if side == 0 else down}, device_id_type=MESH,
        )

    def each(g):
        return slice(g * 2 * ROWS, (g + 1) * 2 * ROWS)

    def accumulate(subs, fresh):
        def one_owner(ahead, carry):
            owner = lax.rem(z + ahead, 4)
            for g in range(8):
                sums = trial_sums(owner, g, subs)
                if fresh:
                    acc[ahead, each(g), :] = sums
                else:
                    acc[ahead, each(g), :] += sums
            return carry

        lax.fori_loop(0, 4, one_owner, 0)

    def last(ahead, g):
        other = (1 - core) * SUBS
        sums = acc[ahead, each(g), :] + trial_sums(lax.rem(z + ahead, 4), g, (other + 2, other + 3))
        return sums[:ROWS], sums[ROWS:]

    def line_of(g):
        return slice(g * ROWS, (g + 1) * ROWS)

    collect(0)
    spread(core, 0)
    forward(0).wait()
    spread(1 - core, 0)
    accumulate((0, 1, 4, 5), True)
    collect(1)
    spread(core, 1)
    accumulate((core * SUBS + 2, core * SUBS + 3), False)
    forward(1).wait()
    spread(1 - core, 1)

    for p in range(2):
        for g in range(4 * p, 4 * p + 4):
            sums = last(2, g)
            for b in range(2):
                chunk[0, b, line_of(g), :] = sums[b].astype(jnp.bfloat16)
        for b in range(2):
            far(b, p).start()

    for side in range(2):
        for g in range(8):
            sums = last(1 + 2 * side, g)
            half[side, line_of(g), :] = sums[side]
            chunk[1 + side, 1 - side, line_of(g), :] = sums[1 - side].astype(jnp.bfloat16)
        direct(side).start()

    for g in range(8):
        sums = last(0, g)
        for b in range(2):
            total[b, line_of(g), :] = sums[b]

    for p in range(2):
        cut = slice(p * 4 * ROWS, (p + 1) * 4 * ROWS)
        for side in range(2):
            far(side, p).wait_recv()
            joined = half[side, cut, :] + relay[side, cut, :].astype(jnp.float32)
            chunk[1 + side, side, cut, :] = joined.astype(jnp.bfloat16)
            close(side, p).start()

    def sent(i, carry):
        outgoing(0, i).wait_send()
        outgoing(1, i).wait_send()
        return carry

    lax.fori_loop(1, NT, sent, 0)

    for side in range(2):
        direct(side).wait()
        for p in range(2):
            far(side, p).wait_send()
            close(side, p).wait()


def finish(total, near, window, roots, series_ref, peaks_ref, summed, flat):
    for b in range(2):
        summed[b] = (
            total[b] + (near[0, b].astype(jnp.float32) + near[1, b].astype(jnp.float32))
        ) * (1.0 / math.sqrt(CH))
    flat[16 * ROWS :, :] = jnp.zeros((16, LANES), jnp.bfloat16)

    for row in range(ROWS):
        pieces = [summed[b, pl.ds(row, 8, stride=ROWS), :] for b in range(2)]
        flat[row * 16 : (row + 1) * 16, :] = jnp.concatenate(pieces, axis=0).astype(jnp.bfloat16)
        for b in range(2):
            series_ref[b, :, row * LANES : (row + 1) * LANES] = pieces[b].astype(jnp.bfloat16)

    best = None
    for part_of in range(4):
        low = part_of * 128
        pair = jnp.concatenate([flat[low : low + 128, :], flat[low + 16 : low + 144, :]], axis=1)
        sums = jnp.dot(pair, window[...], preferred_element_type=jnp.float32)
        for row in range(8):
            piece = sums[row * 16 : (row + 1) * 16]
            best = piece if best is None else jnp.maximum(best, piece)
    for w in range(4):
        cut = slice(w * LANES, (w + 1) * LANES)
        top = jnp.max(best[:, cut].T, axis=0, keepdims=True) / roots[0:1, w * LANES : w * LANES + 16]
        for b in range(2):
            peaks_ref[b, w : w + 1, :] = top[:, b * 8 : (b + 1) * 8]


def local(intensity, fine_delay, span_start, sub_rel, offset, widths):
    vmem = pl.BlockSpec(memory_space=pltpu.VMEM)
    hbm = pl.BlockSpec(memory_space=pltpu.HBM)
    pieces = pl.pallas_call(
        kernel,
        out_shape=(
            jax.ShapeDtypeStruct((2, 8 * ROWS, LANES), jnp.float32),
            jax.ShapeDtypeStruct((2, 2, 8 * ROWS, LANES), jnp.bfloat16),
            jax.ShapeDtypeStruct((2 * LANES, 4 * LANES), jnp.bfloat16),
            jax.ShapeDtypeStruct((8, 4 * LANES), jnp.float32),
        ),
        in_specs=[hbm] * 6,
        out_specs=(vmem,) * 4,
        scratch_shapes=[
            pltpu.VMEM((2, SUBS * CSUB, BLOCK), jnp.bfloat16),
            pltpu.VMEM((SUBS, Q, CSUB), jnp.int32),
            pltpu.SMEM((NT, 32), jnp.int32),
            pltpu.SMEM((8, 64), jnp.int32),
            pltpu.SMEM((8, 64), jnp.int32),
            pltpu.SMEM((4,), jnp.int32),
            pltpu.VMEM((2, 8, 2, BLOCK + 16, LANES), jnp.float32),
            pltpu.VMEM((3, SUBS * Q * 2, LANES), jnp.float32),
            pltpu.VMEM((NT, MSG, LANES), jnp.bfloat16),
            pltpu.VMEM((2, NT + 1, MSG, LANES), jnp.bfloat16),
            pltpu.VMEM((64 * PITCH, LANES), jnp.float32),
            pltpu.VMEM((2, 8 * ROWS, LANES), jnp.bfloat16),
            pltpu.VMEM((3, 2, 8 * ROWS, LANES), jnp.bfloat16),
            pltpu.VMEM((2, 8 * ROWS, LANES), jnp.float32),
            pltpu.VMEM((4, 16 * ROWS, LANES), jnp.float32),
            pltpu.SemaphoreType.DMA((2, SUBS)),
            pltpu.SemaphoreType.DMA((4,)),
            pltpu.SemaphoreType.DMA((2, NT)),
            pltpu.SemaphoreType.DMA((2, NT)),
            pltpu.SemaphoreType.DMA((2,)),
            pltpu.SemaphoreType.DMA((2,)),
            pltpu.SemaphoreType.DMA((10,)),
            pltpu.SemaphoreType.DMA((10,)),
        ],
        compiler_params=pltpu.CompilerParams(
            collective_id=0, has_side_effects=True, vmem_limit_bytes=VMEM_MIB * 1024 * 1024
        ),
        name="dedisperse",
    )(*[
        pltpu.with_memory_space_constraint(a, pltpu.HBM)
        for a in (intensity, fine_delay, span_start, sub_rel.T, offset.T, widths)
    ])
    series, peaks = pl.pallas_call(
        finish,
        out_shape=(
            jax.ShapeDtypeStruct((2, 8, ROWS * LANES), jnp.bfloat16),
            jax.ShapeDtypeStruct((2, 4, 8), jnp.float32),
        ),
        in_specs=[vmem] * 4,
        out_specs=(vmem, vmem),
        scratch_shapes=[
            pltpu.VMEM((2, 8 * ROWS, LANES), jnp.float32),
            pltpu.VMEM((16 * ROWS + 16, LANES), jnp.bfloat16),
        ],
        compiler_params=pltpu.CompilerParams(vmem_limit_bytes=VMEM_MIB * 1024 * 1024),
        name="finish",
    )(*pieces)
    return series, peaks.transpose(0, 2, 1)


def solution(mesh):
    return jax.shard_map(
        local,
        mesh=mesh,
        in_specs=(
            P(None, "band", "trial"),
            P("band", None, None),
            P(),
            P("trial", None),
            P("trial", None),
            P(),
        ),
        out_specs=(P(None, ("trial", "band"), None), P(None, ("trial", "band"), None)),
        check_vma=False,
    )
```

time: 33.3 us -> 28.2 us (0.85)
  local copies, waits for them, and re-layouts: 2.94 us -> 0 us
  Pallas kernels: 29.4 us -> 27.5 us
    pallas_call x1 -> x2, Pallas kernels: 29.4 us -> 27.5 us  [the longest x1 26.2 us: local(): pl.pallas_call(kernel, out_shape=(jax.ShapeDtypeStruct((2, 8 * ROWS, LANE...]
    unnamed x1 -> x0, local copies, waits for them, and re-layouts: 1.57 us -> none
    pallas_call x1 -> x0, local copies, waits for them, and re-layouts: 1.37 us -> none  [local(): pl.pallas_call(kernel, out_shape=(jax.ShapeDtypeStruct((2, 8, ROWS * LANE...]
where the time goes in v2:
time: 28.2 us; the launch traced here: 28.1 us
  Pallas kernels  27.5 us (98%)
  between operations  0.64 us (2%)
    pallas_call x1, Pallas kernels, local(): pl.pallas_call(kernel, out_shape=(jax.ShapeDtypeStruct((2, 8 * ROWS, LANE...  26.2 us
    pallas_call x1, Pallas kernels, local(): pl.pallas_call(finish, out_shape=(jax.ShapeDtypeStruct((2, 8, ROWS * LANE...  1.24 us

profile of v2, /device:TPU:1, one launch (start us, length us, event | category | flops | bytes accessed | tf_op | source)
XLA Modules:
  0.0 28.1 jit_solution(10747790811622014616)
XLA Ops:
  0.6 26.2 %dedisperse.1 = (f32[2,256,128]{2,1,0:T(8,128)S(1)}, bf16[2,2,256,128]{3,2,1,0:T(8,128)(2,1)S(1)}, bf16[256,512]{1,0:T(8,128)(2,1)S(1)}, f32[8,512]{1,0:T(8,128)S(1)}) custom-call(bf16[2,2048,256]{2,1,0:T(8,128)(2,1)} %x_hbm.1, s32[4,32,512]{2,1,0:T(8,128)} %delay_hbm.1, s32[16,32]{1,0:T(8,128)} %span_hbm.1, s32[32,64]{1,0:T(8,128)} %bitcast.3, ...), custom_call_target="tpu_custom_call" | custom-call | tf_op jit(solution)/shard_map/dedisperse/pallas_call | solution.py:415
  26.9 1.2 %finish.1 = (bf16[2,8,4096]{2,1,0:T(8,128)(2,1)}, f32[2,4,8]{2,1,0:T(4,128)}) custom-call(f32[2,256,128]{2,1,0:T(8,128)S(1)} %get-tuple-element.8.total, bf16[2,2,256,128]{3,2,1,0:T(8,128)(2,1)S(1)} %get-tuple-element.9.near, bf16[256,512]{1,0:T(8,128)(2,1)S(1)} %get-tuple-element.10.window, f32[8,512]{1,0:T(8,128)S(1)} %get-tuple-element.11.roots), custom_call_target="tpu_custom_call" | custom-call | tf_op jit(solution)/shard_map/finish/pallas_call | solution.py:458

commit v3 on v2

--- a/solution.py
+++ b/solution.py
@@ -69,14 +69,13 @@
 
     def load(s):
         cut = pl.ds(s * CSUB, CSUB)
-        return (
-            pltpu.make_async_copy(x_hbm.at[:, cut, :], xv.at[:, cut, :], in_sem.at[0, s]),
-            pltpu.make_async_copy(delay_hbm.at[s], dv.at[s], in_sem.at[1, s]),
-        )
-
-    for s in range(SUBS):
-        for copy in load(s):
-            copy.start()
+        return pltpu.make_async_copy(x_hbm.at[:, cut, :], xv.at[:, cut, :], in_sem.at[s])
+
+    delay_copy = pltpu.make_async_copy(delay_hbm, dv, in_sem.at[SUBS])
+    load(0).start()
+    delay_copy.start()
+    for s in range(1, SUBS):
+        load(s).start()
 
     def greet(i, carry):
         pl.semaphore_signal(barrier, inc=1, device_id={"trial": lax.rem(me + i, NT)}, device_id_type=MESH)
@@ -107,24 +106,34 @@
             both = [part[h, pl.ds(start, 8), :] for start in starts]
             put(pair * 40 + h * 16, jnp.concatenate(both, axis=0).astype(jnp.bfloat16))
         early = [part[2, pl.ds(start, 8), :] for start in starts]
-        put(pair * 40 + 32, (pltpu.roll(early[0], 96, 1) + early[1]).astype(jnp.bfloat16))
+        put(pair * 40 + 32, (early[0] + early[1]).astype(jnp.bfloat16))
 
     def outgoing(pair, i):
         cut = pl.ds(pair * 40, 40)
         return pltpu.make_async_remote_copy(
             src_ref=send.at[i, cut, :], dst_ref=recv.at[core, me, cut, :],
-            send_sem=send_sem.at[pair, i], recv_sem=recv_sem.at[pair, i],
+            send_sem=send_sem.at[pair], recv_sem=recv_sem.at[pair],
             device_id={"trial": lax.rem(me + i, NT)}, device_id_type=MESH,
         )
 
+    def all_of(pair):
+        cut = pl.ds(pair * 40, 40)
+        return pltpu.make_async_remote_copy(
+            src_ref=send.at[pl.ds(1, NT - 1), cut, :], dst_ref=recv.at[core, pl.ds(0, NT - 1), cut, :],
+            send_sem=send_sem.at[pair], recv_sem=recv_sem.at[pair],
+            device_id={"trial": lax.rem(me + 1, NT)}, device_id_type=MESH,
+        )
+
     def send_pair(pair):
-        for i in FAR_FIRST:
-
-            def put(row, value):
-                send[i, row : row + value.shape[0], :] = value
-
-            gather(pair, lax.rem(me + i, NT), put)
-            outgoing(pair, i).start()
+        for first in range(0, NT - 1, 5):
+            for i in FAR_FIRST[first : first + 5]:
+
+                def put(row, value):
+                    send[i, row : row + value.shape[0], :] = value
+
+                gather(pair, lax.rem(me + i, NT), put)
+            for i in FAR_FIRST[first : first + 5]:
+                outgoing(pair, i).start()
 
         def put_own(row, value):
             recv[core, me, row : row + value.shape[0], :] = value
@@ -146,7 +155,7 @@
     def turn_delays(s):
         delays = dv[s].astype(jnp.float32)
         delays = jnp.concatenate([delays - 8.0 * j for j in range(4)], axis=0)
-        lagged[s] = delays.T.astype(jnp.bfloat16)
+        lagged[s] = delays.astype(jnp.bfloat16).T
 
     def product(s, m):
         delays = lagged[s]
@@ -182,42 +191,47 @@
             return picked
 
         for tile in range(3):
-            turned = jnp.concatenate([line(16 * tile - 15 + i) for i in range(16)], axis=0).T
+            lines = [line(16 * tile - 15 + i) for i in range(16)]
+            if tile == 0 and s % 2 == 0:
+                lines = lines[4:] + [blank] * 4
+            turned = jnp.concatenate(lines, axis=0).T
             folded = (turned[0:32] + turned[32:64]) + (turned[64:96] + turned[96:128])
             part[(tile + 2) % 3, pl.ds(s * 64 + b, 32, stride=2), :] = folded
 
     def arrive(s):
-        for copy in load(s):
-            copy.wait()
+        load(s).wait()
 
     arrive(0)
+    delay_copy.wait()
     turn_data(0, 0)
     turn_data(0, 1)
     turn_delays(0)
     for s in range(SUBS):
+        product(s, 0)
+        if s in (1, 3):
+            fold(s - 1, 0)
+        if s == 2:
+            fold(1, 0)
+            fold(1, 1)
+        product(s, 2)
+        if s == 2:
+            for copy in small:
+                copy.wait()
+            pl.semaphore_wait(barrier, NT + 2)
+            send_pair(0)
         if s + 1 < SUBS:
             arrive(s + 1)
-        product(s, 0)
-        if s % 2 == 1:
-            fold(s - 1, 0)
-        product(s, 2)
-        if s + 1 < SUBS:
             turn_data(s + 1, 0)
         product(s, 4)
-        if s % 2 == 1:
+        if s in (1, 3):
             fold(s - 1, 1)
         product(s, 6)
         if s + 1 < SUBS:
             turn_data(s + 1, 1)
             turn_delays(s + 1)
-        if s % 2 == 1:
-            fold(s, 0)
-            fold(s, 1)
-            if s == 1:
-                for copy in small:
-                    copy.wait()
-                pl.semaphore_wait(barrier, NT + 2)
-            send_pair(s // 2)
+    fold(SUBS - 1, 0)
+    fold(SUBS - 1, 1)
+    send_pair(1)
 
     def forward(pair):
         cut = (core, pl.ds(0, NT), pl.ds(pair * 40, 40))
@@ -228,11 +242,7 @@
         )
 
     def collect(pair):
-        def wait_one(i, carry):
-            outgoing(pair, i).wait_recv()
-            return carry
-
-        lax.fori_loop(1, NT, wait_one, 0)
+        all_of(pair).wait_recv()
         forward(pair).start()
 
     def spread(c, pair):
@@ -285,7 +295,7 @@
         where, cut = piece(b, p)
         return pltpu.make_async_remote_copy(
             src_ref=chunk.at[0, b, cut, :], dst_ref=relay.at[b, cut, :],
-            send_sem=zsend_sem.at[2 * b + p], recv_sem=zrecv_sem.at[2 * b + p],
+            send_sem=zsend_sem.at[0], recv_sem=zrecv_sem.at[2 * b + p],
             device_id=where, device_id_type=MESH,
         )
 
@@ -293,36 +303,43 @@
         where, cut = piece(side, p)
         return pltpu.make_async_remote_copy(
             src_ref=chunk.at[1 + side, side, cut, :], dst_ref=near.at[side, side, cut, :],
-            send_sem=zsend_sem.at[4 + 2 * side + p], recv_sem=zrecv_sem.at[4 + 2 * side + p],
+            send_sem=zsend_sem.at[0], recv_sem=zrecv_sem.at[4 + 2 * side + p],
             device_id=where, device_id_type=MESH,
         )
 
     def direct(side):
         return pltpu.make_async_remote_copy(
             src_ref=chunk.at[1 + side, 1 - side], dst_ref=near.at[side, 1 - side],
-            send_sem=zsend_sem.at[8 + side], recv_sem=zrecv_sem.at[8 + side],
+            send_sem=zsend_sem.at[0], recv_sem=zrecv_sem.at[8 + side],
             device_id={"band": up if side == 0 else down}, device_id_type=MESH,
         )
 
     def each(g):
         return slice(g * 2 * ROWS, (g + 1) * 2 * ROWS)
 
-    def accumulate(subs, fresh):
-        def one_owner(ahead, carry):
-            owner = lax.rem(z + ahead, 4)
-            for g in range(8):
-                sums = trial_sums(owner, g, subs)
-                if fresh:
-                    acc[ahead, each(g), :] = sums
-                else:
-                    acc[ahead, each(g), :] += sums
-            return carry
-
-        lax.fori_loop(0, 4, one_owner, 0)
+    def of(c, pair):
+        return (c * SUBS + 2 * pair, c * SUBS + 2 * pair + 1)
+
+    sib = 1 - core
+
+    def first_part(ahead, carry):
+        for g in range(8):
+            acc[ahead, each(g), :] = trial_sums(lax.rem(z + ahead, 4), g, of(core, 0))
+        return carry
+
+    def more_of(ahead, subs):
+        for g in range(8):
+            acc[ahead, each(g), :] += trial_sums(lax.rem(z + ahead, 4), g, subs)
+
+    rest = {
+        2: of(sib, 1),
+        1: (2, 3, 6, 7),
+        3: of(sib, 0) + (2, 3, 6, 7),
+        0: of(sib, 0) + (2, 3, 6, 7),
+    }
 
     def last(ahead, g):
-        other = (1 - core) * SUBS
-        sums = acc[ahead, each(g), :] + trial_sums(lax.rem(z + ahead, 4), g, (other + 2, other + 3))
+        sums = acc[ahead, each(g), :] + trial_sums(lax.rem(z + ahead, 4), g, rest[ahead])
         return sums[:ROWS], sums[ROWS:]
 
     def line_of(g):
@@ -330,14 +347,16 @@
 
     collect(0)
     spread(core, 0)
+    lax.fori_loop(0, 4, first_part, 0)
     forward(0).wait()
-    spread(1 - core, 0)
-    accumulate((0, 1, 4, 5), True)
+    spread(sib, 0)
+    more_of(2, of(sib, 0))
     collect(1)
     spread(core, 1)
-    accumulate((core * SUBS + 2, core * SUBS + 3), False)
+    more_of(2, of(core, 1))
+    more_of(1, of(sib, 0))
     forward(1).wait()
-    spread(1 - core, 1)
+    spread(sib, 1)
 
     for p in range(2):
         for g in range(4 * p, 4 * p + 4):
@@ -367,41 +386,37 @@
             chunk[1 + side, side, cut, :] = joined.astype(jnp.bfloat16)
             close(side, p).start()
 
-    def sent(i, carry):
-        outgoing(0, i).wait_send()
-        outgoing(1, i).wait_send()
-        return carry
-
-    lax.fori_loop(1, NT, sent, 0)
-
+    for pair in range(2):
+        all_of(pair).wait_send()
     for side in range(2):
-        direct(side).wait()
+        direct(side).wait_recv()
         for p in range(2):
-            far(side, p).wait_send()
-            close(side, p).wait()
-
-
-def finish(total, near, window, roots, series_ref, peaks_ref, summed, flat):
+            close(side, p).wait_recv()
+    pltpu.make_async_remote_copy(
+        src_ref=chunk, dst_ref=chunk, send_sem=zsend_sem.at[0], recv_sem=zrecv_sem.at[0],
+        device_id={"band": up}, device_id_type=MESH,
+    ).wait_send()
+
+
+def finish(total, near, window, roots, series_ref, peaks_ref, summed):
     for b in range(2):
         summed[b] = (
             total[b] + (near[0, b].astype(jnp.float32) + near[1, b].astype(jnp.float32))
         ) * (1.0 / math.sqrt(CH))
-    flat[16 * ROWS :, :] = jnp.zeros((16, LANES), jnp.bfloat16)
-
+
+    flat = []
     for row in range(ROWS):
         pieces = [summed[b, pl.ds(row, 8, stride=ROWS), :] for b in range(2)]
-        flat[row * 16 : (row + 1) * 16, :] = jnp.concatenate(pieces, axis=0).astype(jnp.bfloat16)
+        flat.append(jnp.concatenate(pieces, axis=0).astype(jnp.bfloat16))
         for b in range(2):
             series_ref[b, :, row * LANES : (row + 1) * LANES] = pieces[b].astype(jnp.bfloat16)
-
-    best = None
-    for part_of in range(4):
-        low = part_of * 128
-        pair = jnp.concatenate([flat[low : low + 128, :], flat[low + 16 : low + 144, :]], axis=1)
-        sums = jnp.dot(pair, window[...], preferred_element_type=jnp.float32)
-        for row in range(8):
-            piece = sums[row * 16 : (row + 1) * 16]
-            best = piece if best is None else jnp.maximum(best, piece)
+    flat.append(jnp.zeros((16, LANES), jnp.bfloat16))
+
+    halves = [jnp.concatenate(flat[i : i + ROWS], axis=0) for i in range(2)]
+    sums = jnp.dot(jnp.concatenate(halves, axis=1), window[...], preferred_element_type=jnp.float32)
+    best = sums[0:16]
+    for row in range(1, ROWS):
+        best = jnp.maximum(best, sums[row * 16 : (row + 1) * 16])
     for w in range(4):
         cut = slice(w * LANES, (w + 1) * LANES)
         top = jnp.max(best[:, cut].T, axis=0, keepdims=True) / roots[0:1, w * LANES : w * LANES + 16]
@@ -438,13 +453,13 @@
             pltpu.VMEM((3, 2, 8 * ROWS, LANES), jnp.bfloat16),
             pltpu.VMEM((2, 8 * ROWS, LANES), jnp.float32),
             pltpu.VMEM((4, 16 * ROWS, LANES), jnp.float32),
-            pltpu.SemaphoreType.DMA((2, SUBS)),
+            pltpu.SemaphoreType.DMA((SUBS + 1,)),
             pltpu.SemaphoreType.DMA((4,)),
-            pltpu.SemaphoreType.DMA((2, NT)),
-            pltpu.SemaphoreType.DMA((2, NT)),
             pltpu.SemaphoreType.DMA((2,)),
             pltpu.SemaphoreType.DMA((2,)),
-            pltpu.SemaphoreType.DMA((10,)),
+            pltpu.SemaphoreType.DMA((2,)),
+            pltpu.SemaphoreType.DMA((2,)),
+            pltpu.SemaphoreType.DMA((1,)),
             pltpu.SemaphoreType.DMA((10,)),
         ],
         compiler_params=pltpu.CompilerParams(
@@ -465,7 +480,6 @@
         out_specs=(vmem, vmem),
         scratch_shapes=[
             pltpu.VMEM((2, 8 * ROWS, LANES), jnp.float32),
-            pltpu.VMEM((16 * ROWS + 16, LANES), jnp.bfloat16),
         ],
         compiler_params=pltpu.CompilerParams(vmem_limit_bytes=VMEM_MIB * 1024 * 1024),
         name="finish",

time: 28.2 us -> 26.4 us (0.936)
  Pallas kernels: 27.5 us -> 25.7 us
    pallas_call x1, Pallas kernels: 26.2 us -> 24.5 us  [local(): pl.pallas_call(kernel, out_shape=(jax.ShapeDtypeStruct((2, 8 * ROWS, LANE...]
where the time goes in v3:
time: 26.4 us; the launch traced here: 26.3 us
  Pallas kernels  25.7 us (97%)
  between operations  0.64 us (2%)
    pallas_call x1, Pallas kernels, local(): pl.pallas_call(kernel, out_shape=(jax.ShapeDtypeStruct((2, 8 * ROWS, LANE...  24.5 us
    pallas_call x1, Pallas kernels, local(): pl.pallas_call(finish, out_shape=(jax.ShapeDtypeStruct((2, 8, ROWS * LANE...  1.2 us

profile of v3, /device:TPU:1, one launch (start us, length us, event | category | flops | bytes accessed | tf_op | source)
XLA Modules:
  0.0 26.3 jit_solution(18035504573914315201)
XLA Ops:
  0.6 24.5 %dedisperse.1 = (f32[2,256,128]{2,1,0:T(8,128)S(1)}, bf16[2,2,256,128]{3,2,1,0:T(8,128)(2,1)S(1)}, bf16[256,512]{1,0:T(8,128)(2,1)S(1)}, f32[8,512]{1,0:T(8,128)S(1)}) custom-call(bf16[2,2048,256]{2,1,0:T(8,128)(2,1)} %x_hbm.1, s32[4,32,512]{2,1,0:T(8,128)} %delay_hbm.1, s32[16,32]{1,0:T(8,128)} %span_hbm.1, s32[32,64]{1,0:T(8,128)} %bitcast.3, ...), custom_call_target="tpu_custom_call" | custom-call | tf_op jit(solution)/shard_map/dedisperse/pallas_call | solution.py:430
  25.1 1.2 %finish.1 = (bf16[2,8,4096]{2,1,0:T(8,128)(2,1)}, f32[2,4,8]{2,1,0:T(4,128)}) custom-call(f32[2,256,128]{2,1,0:T(8,128)S(1)} %get-tuple-element.8.total, bf16[2,2,256,128]{3,2,1,0:T(8,128)(2,1)S(1)} %get-tuple-element.9.near, bf16[256,512]{1,0:T(8,128)(2,1)S(1)} %get-tuple-element.10.window, f32[8,512]{1,0:T(8,128)S(1)} %get-tuple-element.11.roots), custom_call_target="tpu_custom_call" | custom-call | tf_op jit(solution)/shard_map/finish/pallas_call | solution.py:473
